TPU v7x, 32 devices: a whole 2x2x4 slice. The times are simulated.
32 devices in a mesh: dp: 8 (over y, x, core), tensor: 4 (over z).
Axes of the slice: x: 2, y: 2, z: 4, core: 2. Of those that a mesh axis runs over, the one named last changes fastest.
Arguments:
- hidden_in: bfloat16 [4096, 1536], P(('dp', 'tensor')), may hold values from -6 to 6
- positions: int32 [4096], P(('dp', 'tensor')), may hold values from 0 to 511, as said below
- gain_attn: bfloat16 [1536], P(('dp', 'tensor')), may hold values from 0.5 to 1.5
- w_query: bfloat16 [1536, 1536], P(('dp', 'tensor')), may hold values from -0.15625 to 0.15625
- key_matrix: bfloat16 [1536, 768], P(('dp', 'tensor')), may hold values from -0.15625 to 0.15625
- value_matrix: bfloat16 [1536, 768], P(('dp', 'tensor')), may hold values from -0.15625 to 0.15625
- w_output: bfloat16 [1536, 1536], P(('dp', 'tensor')), may hold values from -3.5 to 3.5
- gain_mlp: bfloat16 [1536], P(('dp', 'tensor')), may hold values from 0.5 to 1.5
- w_gate: bfloat16 [1536, 4096], P(None, 'tensor'), may hold values from -0.15625 to 0.15625
- w_up: bfloat16 [1536, 4096], P(None, 'tensor'), may hold values from -0.15625 to 0.15625
- w_down: bfloat16 [4096, 1536], P('tensor'), may hold values from -0.09375 to 0.09375
- cotangent: bfloat16 [4096, 1536], P(('dp', 'tensor')), may hold values from -6 to 6
Outputs:
- layer_out: bfloat16 [4096, 1536], P(('dp', 'tensor'))
- grad_input: float32 [4096, 1536], P(('dp', 'tensor'))
- grad_gain_attn: float32 [1536], P(('dp', 'tensor'))
- grad_w_query: float32 [1536, 1536], P(('dp', 'tensor'))
- grad_w_key: float32 [1536, 768], P(('dp', 'tensor'))
- grad_w_value: float32 [1536, 768], P(('dp', 'tensor'))
- grad_w_output: float32 [1536, 1536], P(('dp', 'tensor'))
- grad_gain_mlp: float32 [1536], P(('dp', 'tensor'))
- grad_w_gate: float32 [1536, 4096], P('dp', 'tensor')
- grad_w_up: float32 [1536, 4096], P('dp', 'tensor')
- grad_w_down: float32 [4096, 1536], P('tensor', 'dp')
Inputs may be any that keep to these rules, and one draw needn't show every extreme that they name: positions is 0 at the first token of every document and at every sequence's first row (multiples of 512), and rises by one from each token to the next within a document; documents are runs of consecutive tokens; the first sequence is a single document of 512 tokens.
All inputs are finite; a program needn't handle non-finite values.
Results may differ from a plain program's by a relative error of at most 0.015.
Values may be sent and summed in bfloat16 or wider, within the bound.
A program may use at most 192 MiB of HBM per device.

v0:
```python
import math
import jax
import jax.numpy as jnp
from jax import lax
from jax.sharding import PartitionSpec as P

QUERY_HEADS = 16
KEY_VALUE_HEADS = 8
HEAD_DIMENSION = 96
EPSILON = 1e-05
ROPE_BASE = 100000.0
MASKED = -1e30


def angle_tables(pos_rows, head_size):
    half_size = head_size // 2
    freq_rates = ROPE_BASE ** (-(jnp.arange(half_size, dtype=jnp.float32) * 2.0) / head_size)
    turned = pos_rows.astype(jnp.float32)[:, None] * freq_rates[None, :]
    return (jnp.cos(turned)[:, None, :], jnp.sin(turned)[:, None, :])


def apply_rotary(tensor_in, cosine_table, sine_table):
    half_size = tensor_in.shape[-1] // 2
    lo_half = tensor_in[..., :half_size]
    hi_half = tensor_in[..., half_size:]
    return jnp.concatenate(
        [
            lo_half * cosine_table - hi_half * sine_table,
            hi_half * cosine_table + lo_half * sine_table,
        ],
        axis=-1,
    )


def shards(
    hidden_in,
    positions,
    gain_attn,
    w_query,
    key_matrix,
    value_matrix,
    w_output,
    gain_mlp,
    w_gate,
    w_up,
    w_down,
    cotangent,
):
    tok_rows = hidden_in.shape[0]
    model_width = hidden_in.shape[1]
    num_heads = QUERY_HEADS
    key_value_count = KEY_VALUE_HEADS
    head_size = HEAD_DIMENSION
    kv_width = key_value_count * head_size
    queries_per_group = num_heads // key_value_count
    seq_len = tok_rows * lax.axis_size("tensor")
    score_scale = 1.0 / math.sqrt(head_size)
    gathered = (
        lax.all_gather(gain_attn, ("dp", "tensor"), axis=0, tiled=True),
        lax.all_gather(w_query, ("dp", "tensor"), axis=0, tiled=True),
        lax.all_gather(key_matrix, ("dp", "tensor"), axis=0, tiled=True),
        lax.all_gather(value_matrix, ("dp", "tensor"), axis=0, tiled=True),
        lax.all_gather(w_output, ("dp", "tensor"), axis=0, tiled=True),
        lax.all_gather(gain_mlp, ("dp", "tensor"), axis=0, tiled=True),
    )
    gain_one, query_full, key_full, value_full, output_full, gain_two = gathered
    gain_one_f = gain_one.astype(jnp.float32)
    gain_two_f = gain_two.astype(jnp.float32)
    x_float = hidden_in.astype(jnp.float32)
    inv_one = lax.rsqrt(jnp.mean(x_float * x_float, axis=-1, keepdims=True) + EPSILON)
    normed_one = (x_float * inv_one * gain_one_f).astype(jnp.bfloat16)
    queries = jnp.dot(normed_one, query_full, preferred_element_type=jnp.float32)
    key_projected = jnp.dot(normed_one, key_full, preferred_element_type=jnp.float32)
    value_proj = jnp.dot(normed_one, value_full, preferred_element_type=jnp.float32)
    cosine_table, sine_table = angle_tables(positions, head_size)
    rotated_query_rows = apply_rotary(
        queries.reshape(tok_rows, num_heads, head_size), cosine_table, sine_table
    ).astype(jnp.bfloat16)
    rotated_key_rows = (
        apply_rotary(
            key_projected.reshape(tok_rows, key_value_count, head_size), cosine_table, sine_table
        )
        .astype(jnp.bfloat16)
        .reshape(tok_rows, kv_width)
    )
    value_rows_lowered = value_proj.astype(jnp.bfloat16)
    keys_all, values_all = (
        lax.all_gather(rotated_key_rows, "tensor", axis=0, tiled=True),
        lax.all_gather(value_rows_lowered, "tensor", axis=0, tiled=True),
    )
    offset = lax.axis_index("tensor") * tok_rows
    query_index = offset + jnp.arange(tok_rows, dtype=jnp.int32)
    key_index = jnp.arange(seq_len, dtype=jnp.int32)
    visible = (key_index[None, :] <= query_index[:, None]) & (
        key_index[None, :] >= (query_index - positions)[:, None]
    )
    visible = jnp.tile(visible, (queries_per_group, 1))

    def split_queries(tensor_in):
        return (
            tensor_in.reshape(tok_rows, key_value_count, queries_per_group, head_size)
            .transpose(1, 2, 0, 3)
            .reshape(key_value_count, queries_per_group * tok_rows, head_size)
        )

    def split_keys(tensor_in):
        return tensor_in.reshape(seq_len, key_value_count, head_size).transpose(1, 0, 2)

    def merge_heads(tensor_in):
        return (
            tensor_in.reshape(key_value_count, queries_per_group, tok_rows, head_size)
            .transpose(2, 0, 1, 3)
            .reshape(tok_rows, model_width)
        )

    query_heads = split_queries(rotated_query_rows)
    k_heads = split_keys(keys_all)
    value_heads = split_keys(values_all)

    def attend(head_items):
        q_block, k_block, v_block = head_items
        scores = (
            jnp.einsum("qd,kd->qk", q_block, k_block, preferred_element_type=jnp.float32)
            * score_scale
        )
        scores = jnp.where(visible, scores, MASKED)
        peak = jnp.max(scores, axis=-1, keepdims=True)
        exp_vals = jnp.exp(scores - peak)
        total = jnp.sum(exp_vals, axis=-1, keepdims=True)
        probs = exp_vals / total
        out_block = jnp.einsum(
            "qk,kd->qd", probs.astype(jnp.bfloat16), v_block, preferred_element_type=jnp.float32
        )
        return (out_block, peak[:, 0] + jnp.log(total[:, 0]))

    attended_rows, log_total = lax.map(attend, (query_heads, k_heads, value_heads))
    attended_low = merge_heads(attended_rows).astype(jnp.bfloat16)
    resid_sum = x_float + jnp.dot(attended_low, output_full, preferred_element_type=jnp.float32)
    inv_two = lax.rsqrt(jnp.mean(resid_sum * resid_sum, axis=-1, keepdims=True) + EPSILON)
    normed_two = (resid_sum * inv_two * gain_two_f).astype(jnp.bfloat16)
    rows_all = lax.all_gather(normed_two, "tensor", axis=0, tiled=True)
    gate_val = jnp.dot(rows_all, w_gate, preferred_element_type=jnp.float32)
    up_val = jnp.dot(rows_all, w_up, preferred_element_type=jnp.float32)
    sig_gate = jax.nn.sigmoid(gate_val)
    silu_gate = gate_val * sig_gate
    act_low = (silu_gate * up_val).astype(jnp.bfloat16)
    mlp_sum = lax.psum_scatter(
        jnp.dot(act_low, w_down, preferred_element_type=jnp.float32).astype(jnp.bfloat16),
        "tensor",
        scatter_dimension=0,
        tiled=True,
    ).astype(jnp.float32)
    layer_out = (resid_sum + mlp_sum).astype(jnp.bfloat16)
    grad_float = cotangent.astype(jnp.float32)
    grad_all = lax.all_gather(cotangent, "tensor", axis=0, tiled=True)
    grad_down = jnp.einsum("sf,sd->fd", act_low, grad_all, preferred_element_type=jnp.float32)
    g_act = jnp.einsum("sd,fd->sf", grad_all, w_down, preferred_element_type=jnp.float32)
    g_gate = (g_act * up_val * sig_gate * (1.0 + gate_val * (1.0 - sig_gate))).astype(jnp.bfloat16)
    g_up = (g_act * silu_gate).astype(jnp.bfloat16)
    grad_gate = jnp.einsum("sd,sf->df", rows_all, g_gate, preferred_element_type=jnp.float32)
    grad_up = jnp.einsum("sd,sf->df", rows_all, g_up, preferred_element_type=jnp.float32)
    g_norm_two = lax.psum_scatter(
        (
            jnp.einsum("sf,df->sd", g_gate, w_gate, preferred_element_type=jnp.float32)
            + jnp.einsum("sf,df->sd", g_up, w_up, preferred_element_type=jnp.float32)
        ).astype(jnp.bfloat16),
        "tensor",
        scatter_dimension=0,
        tiled=True,
    ).astype(jnp.float32)
    scaled_two = gain_two_f * g_norm_two
    grad_gain_two = jnp.sum(g_norm_two * resid_sum * inv_two, axis=0)
    g_resid = (
        grad_float
        + inv_two * scaled_two
        - resid_sum * inv_two**3 * jnp.mean(scaled_two * resid_sum, axis=-1, keepdims=True)
    )
    g_resid_low = g_resid.astype(jnp.bfloat16)
    grad_output = jnp.einsum(
        "tc,td->cd", attended_low, g_resid_low, preferred_element_type=jnp.float32
    )
    g_att = jnp.einsum(
        "td,cd->tc", g_resid_low, output_full, preferred_element_type=jnp.float32
    ).astype(jnp.bfloat16)
    g_heads = split_queries(g_att)

    def attend_back(head_items):
        q_block, k_block, v_block, log_block, g_block = head_items
        scores = (
            jnp.einsum("qd,kd->qk", q_block, k_block, preferred_element_type=jnp.float32)
            * score_scale
        )
        scores = jnp.where(visible, scores, MASKED)
        probs = jnp.exp(scores - log_block[:, None])
        g_probs = jnp.einsum("qd,kd->qk", g_block, v_block, preferred_element_type=jnp.float32)
        g_scores = (probs * (g_probs - jnp.sum(probs * g_probs, axis=-1, keepdims=True))).astype(
            jnp.bfloat16
        )
        g_rq = (
            jnp.einsum("qk,kd->qd", g_scores, k_block, preferred_element_type=jnp.float32)
            * score_scale
        )
        g_rk = (
            jnp.einsum("qk,qd->kd", g_scores, q_block, preferred_element_type=jnp.float32)
            * score_scale
        )
        g_val = jnp.einsum(
            "qk,qd->kd", probs.astype(jnp.bfloat16), g_block, preferred_element_type=jnp.float32
        )
        return (g_rq, g_rk, g_val)

    g_rq, g_rk, g_val = lax.map(
        attend_back, (query_heads, k_heads, value_heads, log_total, g_heads)
    )
    g_rk_flat = g_rk.transpose(1, 0, 2).reshape(seq_len, kv_width)
    g_val_flat = g_val.transpose(1, 0, 2).reshape(seq_len, kv_width)
    key_part, value_part = (
        lax.psum_scatter(
            g_rk_flat.astype(jnp.bfloat16), "tensor", scatter_dimension=0, tiled=True
        ).astype(jnp.float32),
        lax.psum_scatter(
            g_val_flat.astype(jnp.bfloat16), "tensor", scatter_dimension=0, tiled=True
        ).astype(jnp.float32),
    )
    g_queries = (
        apply_rotary(
            merge_heads(g_rq).reshape(tok_rows, num_heads, head_size), cosine_table, -sine_table
        )
        .reshape(tok_rows, model_width)
        .astype(jnp.bfloat16)
    )
    g_keys = (
        apply_rotary(
            key_part.reshape(tok_rows, key_value_count, head_size), cosine_table, -sine_table
        )
        .reshape(tok_rows, kv_width)
        .astype(jnp.bfloat16)
    )
    g_values = value_part.astype(jnp.bfloat16)
    grad_query = jnp.einsum("tc,td->cd", normed_one, g_queries, preferred_element_type=jnp.float32)
    grad_key = jnp.einsum("tc,td->cd", normed_one, g_keys, preferred_element_type=jnp.float32)
    grad_value = jnp.einsum("tc,td->cd", normed_one, g_values, preferred_element_type=jnp.float32)
    g_norm_one = (
        jnp.einsum("td,cd->tc", g_queries, query_full, preferred_element_type=jnp.float32)
        + jnp.einsum("td,cd->tc", g_keys, key_full, preferred_element_type=jnp.float32)
        + jnp.einsum("td,cd->tc", g_values, value_full, preferred_element_type=jnp.float32)
    )
    scaled_one = gain_one_f * g_norm_one
    grad_gain_one = jnp.sum(g_norm_one * x_float * inv_one, axis=0)
    grad_input = (
        g_resid
        + inv_one * scaled_one
        - x_float * inv_one**3 * jnp.mean(scaled_one * x_float, axis=-1, keepdims=True)
    )
    query_part, keyw_part, valuew_part, out_part, gain_one_part, gain_two_part = (
        lax.psum_scatter(grad_query, ("dp", "tensor"), scatter_dimension=0, tiled=True),
        lax.psum_scatter(grad_key, ("dp", "tensor"), scatter_dimension=0, tiled=True),
        lax.psum_scatter(grad_value, ("dp", "tensor"), scatter_dimension=0, tiled=True),
        lax.psum_scatter(grad_output, ("dp", "tensor"), scatter_dimension=0, tiled=True),
        lax.psum_scatter(grad_gain_one, ("dp", "tensor"), scatter_dimension=0, tiled=True),
        lax.psum_scatter(grad_gain_two, ("dp", "tensor"), scatter_dimension=0, tiled=True),
    )
    gate_sum, up_sum, down_sum = (
        lax.psum_scatter(grad_gate, "dp", scatter_dimension=0, tiled=True),
        lax.psum_scatter(grad_up, "dp", scatter_dimension=0, tiled=True),
        lax.psum_scatter(grad_down, "dp", scatter_dimension=1, tiled=True),
    )
    return (
        layer_out,
        grad_input,
        gain_one_part,
        query_part,
        keyw_part,
        valuew_part,
        out_part,
        gain_two_part,
        gate_sum,
        up_sum,
        down_sum,
    )


def solution(mesh):
    placed = (
        P(("dp", "tensor"), None),
        P(("dp", "tensor")),
        P(("dp", "tensor")),
        P(("dp", "tensor"), None),
        P(("dp", "tensor"), None),
        P(("dp", "tensor"), None),
        P(("dp", "tensor"), None),
        P(("dp", "tensor")),
        P(None, "tensor"),
        P(None, "tensor"),
        P("tensor", None),
        P(("dp", "tensor"), None),
    )
    return jax.shard_map(
        shards,
        mesh=mesh,
        in_specs=placed,
        out_specs=(
            P(("dp", "tensor"), None),
            P(("dp", "tensor"), None),
            P(("dp", "tensor")),
            P(("dp", "tensor"), None),
            P(("dp", "tensor"), None),
            P(("dp", "tensor"), None),
            P(("dp", "tensor"), None),
            P(("dp", "tensor")),
            P("dp", "tensor"),
            P("dp", "tensor"),
            P("tensor", "dp"),
        ),
        check_vma=False,
    )
```

profile of v0, /device:TPU:0, one launch (start us, length us, event | category | flops | bytes accessed | tf_op | source)
XLA Modules:
  0.0 1255.0 jit_solution(6569822728411166291)
XLA Ops:
  12.6 42.1 %all-reduce.5 = (bf16[1536]{0:T(1024)(128)(2,1)S(1)}, bf16[1536]{0:T(1024)(128)(2,1)S(1)}) all-reduce(bf16[1536]{0:T(1024)(128)(2,1)S(1)} %dynamic-update-slice, bf16[1536]{0:T(1024)(128)(2,1)S(1)} %dynamic-update-slice.1), channel_id=1, replica_groups=mesh['dp'=8,'tensor'=4] {'dp','tensor'}, use_global_device_ids=true, to_apply=%add | all-reduce | flops 3072 | bytes 12288
  58.7 11.9 all-gather.9.cloned.1.call-done
  70.6 2.9 fusion.76
  73.7 19.5 %all_gather.33 = bf16[512,768]{0,1:T(8,128)(2,1)} all-gather(bf16[128,768]{0,1:T(8,128)(2,1)S(1)} %bitcast.215), channel_id=1, replica_groups=mesh['dp'=8,'tensor'=4] {'tensor'}, dimensions={0}, use_global_device_ids=true | all-gather | bytes 983040 | tf_op jit(solution)/shard_map/all_gather | solution.py:88
  93.1 2.2 copy.56
  95.4 35.9 %all-gather.11.cloned.1.call-done = bf16[1536,768]{1,0:T(8,128)(2,1)} async-done(((bf16[48,768]{1,0:T(8,128)(2,1)}), bf16[1536,768]{1,0:T(8,128)(2,1)}) %all-gather.11.cloned.1.call-update) | async-done | bytes 2359312 | tf_op jit(solution)/shard_map/all_gather | solution.py:62
  131.3 2.2 convolution_convert_fusion.2
  133.5 21.3 %all_gather.35 = bf16[512,768]{1,0:T(8,128)(2,1)} all-gather(bf16[128,768]{1,0:T(8,128)(2,1)S(1)} %convolution_convert_fusion.2), channel_id=1, replica_groups=mesh['dp'=8,'tensor'=4] {'tensor'}, dimensions={0}, use_global_device_ids=true | all-gather | bytes 983040 | tf_op jit(solution)/shard_map/all_gather | solution.py:89
  154.8 2.3 copy.55
  157.1 2.2 copy.57
  159.3 38.5 %all-gather.7.cloned.1.call-done = bf16[1536,1536]{1,0:T(8,128)(2,1)} async-done(((bf16[48,1536]{1,0:T(8,128)(2,1)}), bf16[1536,1536]{1,0:T(8,128)(2,1)}) %all-gather.7.cloned.1.call-update) | async-done | bytes 4718608 | tf_op jit(solution)/shard_map/all_gather | solution.py:60
  197.8 4.3 fusion.78
  203.0 2.0 copy.53
  205.0 48.8 %while.30 = (s32[]{:T(128)}, bf16[8,256,96]{1,2,0:T(8,128)(2,1)}, f32[8,256]{1,0:T(8,128)}, bf16[8,256,96]{2,1,0:T(8,128)(2,1)}, bf16[8,512,96]{2,1,0:T(8,128)(2...) while((s32[]{:T(128)}, bf16[8,256,96]{1,2,0:T(8,128)(2,1)}, ...), condition=%wide.region_4.5_spmd.clone.clone, body=%wide.region_1.4_spmd.clone.sunk.clone | while | flops 51379968 | bytes 2338905 | solution.py:136
  207.4 1.9 fusion.160
  213.5 1.8 fusion.160
  219.6 1.8 fusion.160
  225.7 1.8 fusion.160
  231.8 1.9 fusion.160
  237.9 1.8 fusion.160
  244.0 1.8 fusion.160
  250.1 1.8 fusion.160
  253.9 1.8 convert_element_type.118
  255.7 1.8 copy.58
  257.5 4.9 all-gather.13.cloned.1.call-done
  262.4 3.4 multiply_reduce_fusion.1
  268.5 34.7 %all-gather.15.cloned.1.call-done = bf16[512,1536]{1,0:T(8,128)(2,1)} async-done(((bf16[128,1536]{1,0:T(8,128)(2,1)}), bf16[512,1536]{1,0:T(8,128)(2,1)}) %all-gather.15.cloned.1.call-update) | async-done | bytes 1572880 | tf_op jit(solution)/shard_map/all_gather | solution.py:141
  303.2 5.6 fusion.81
  308.9 3.1 fusion.82
  312.0 28.6 %all-gather.17.cloned.1.call-done = bf16[512,1536]{1,0:T(8,128)(2,1)} async-done(((bf16[128,1536]{1,0:T(8,128)(2,1)}), bf16[512,1536]{1,0:T(8,128)(2,1)}) %all-gather.17.cloned.1.call-update) | async-done | bytes 1572880 | tf_op jit(solution)/shard_map/all_gather | solution.py:155
  340.6 6.3 multiply_convert_fusion.1
  346.9 1.8 fusion.83
  349.5 3.0 fusion.46
  352.6 4.2 convolution_convert_fusion
  357.0 30.1 %reduce-scatter.18.cloned.1.call-done = bf16[128,1536]{1,0:T(8,128)(2,1)} async-done(((bf16[512,1536]{1,0:T(8,128)(2,1)}), bf16[128,1536]{1,0:T(8,128)(2,1)}) %reduce-scatter.18.cloned.1.call-update) | async-done | bytes 393232 | tf_op jit(solution)/shard_map/reduce_scatter | solution.py:162
  387.0 2.1 fusion.54
  389.1 34.5 %reduce-scatter.16.cloned.1.call-done = bf16[128,1536]{1,0:T(8,128)(2,1)} async-done(((bf16[512,1536]{1,0:T(8,128)(2,1)}), bf16[128,1536]{1,0:T(8,128)(2,1)}) %reduce-scatter.16.cloned.1.call-update) | async-done | bytes 393232 | tf_op jit(solution)/shard_map/reduce_scatter | solution.py:147
  423.7 2.2 fusion.51
  425.9 4.3 convolution_convert_fusion.1
  430.7 61.5 %while.31 = (s32[]{:T(128)}, f32[8,256,96]{1,2,0:T(8,128)}, bf16[8,512,96]{1,2,0:T(8,128)(2,1)}, bf16[8,512,96]{1,2,0:T(8,128)(2,1)}, bf16[8,256,96]{2,1,0:T(8,1...) while((s32[]{:T(128)}, f32[8,256,96]{1,2,0:T(8,128)}, ...), condition=%wide.region_11.12_spmd.clone.clone, body=%wide.region_9.11_spmd.clone.sunk.clone | while | flops 127082240 | bytes 5417073 | solution.py:212
  441.7 1.8 fusion.170
  449.4 1.8 fusion.170
  457.1 1.8 fusion.170
  472.4 1.8 fusion.170
  480.1 1.8 fusion.170
  492.2 2.4 copy.68
  496.1 5.9 fusion.85
  503.3 5.9 fusion.86
  510.4 6.0 fusion.87
  518.0 3.1 fusion.71
  521.2 20.4 %reduce-scatter.36.cloned.1.call-done = bf16[128,768]{1,0:T(8,128)(2,1)} async-done(((bf16[512,768]{1,0:T(8,128)(2,1)}), bf16[128,768]{1,0:T(8,128)(2,1)}) %reduce-scatter.36.cloned.1.call-update) | async-done | bytes 196624
  541.6 3.9 fusion.69
  546.9 5.4 fusion.73
  553.4 5.8 fusion.64
  559.2 4.3 fusion.84
  565.3 2.5 fusion.62
  567.7 40.3 %all-reduce.4 = (f32[1536]{0:T(1024)}, f32[1536]{0:T(1024)}) all-reduce(f32[1536]{0:T(1024)} %get-tuple-element.201, f32[1536]{0:T(1024)} %get-tuple-element.199), channel_id=6, replica_groups=mesh['dp'=8,'tensor'=4] {'dp','tensor'}, use_global_device_ids=true, to_apply=%region_16.17.clone | all-reduce | flops 3072 | bytes 24576
  610.6 2.5 fusion.59
  613.1 60.7 %reduce-scatter.30.cloned.1.call-done = f32[192,1024]{1,0:T(8,128)} async-done(((f32[1536,1024]{1,0:T(8,128)}), f32[192,1024]{1,0:T(8,128)}) %reduce-scatter.30.cloned.1.call-update) | async-done | bytes 786448 | tf_op jit(solution)/shard_map/reduce_scatter | solution.py:265
  673.7 65.7 %reduce-scatter.32.cloned.1.call-done = f32[1024,192]{0,1:T(8,128)} async-done(((f32[1024,1536]{0,1:T(8,128)}), f32[1024,192]{0,1:T(8,128)}) %reduce-scatter.32.cloned.1.call-update) | async-done | bytes 786448 | tf_op jit(solution)/shard_map/reduce_scatter | solution.py:266
  739.5 113.5 %reduce-scatter.22.cloned.1.call-done = f32[48,768]{1,0:T(8,128)} async-done(((f32[1536,768]{1,0:T(8,128)}), f32[48,768]{1,0:T(8,128)}) %reduce-scatter.22.cloned.1.call-update) | async-done | bytes 147472 | tf_op jit(solution)/shard_map/reduce_scatter | solution.py:257
  853.0 112.5 %reduce-scatter.24.cloned.1.call-done = f32[48,768]{1,0:T(8,128)} async-done(((f32[1536,768]{1,0:T(8,128)}), f32[48,768]{1,0:T(8,128)}) %reduce-scatter.24.cloned.1.call-update) | async-done | bytes 147472 | tf_op jit(solution)/shard_map/reduce_scatter | solution.py:258
  965.5 141.5 %reduce-scatter.20.cloned.1.call-done = f32[48,1536]{1,0:T(8,128)} async-done(((f32[1536,1536]{1,0:T(8,128)}), f32[48,1536]{1,0:T(8,128)}) %reduce-scatter.20.cloned.1.call-update) | async-done | bytes 294928 | tf_op jit(solution)/shard_map/reduce_scatter | solution.py:256
  1107.0 141.5 %reduce-scatter.26.cloned.1.call-done = f32[48,1536]{1,0:T(8,128)} async-done(((f32[1536,1536]{1,0:T(8,128)}), f32[48,1536]{1,0:T(8,128)}) %reduce-scatter.26.cloned.1.call-update) | async-done | bytes 294928 | tf_op jit(solution)/shard_map/reduce_scatter | solution.py:259
  (242 shorter events, 113.0 us)
Async XLA Ops:
  7.2 333.4 %copy-start = (bf16[1024,1536]{1,0:T(8,128)(2,1)S(1)}, bf16[1024,1536]{1,0:T(8,128)(2,1)}, u32[]{:S(2)}) copy-start(bf16[1024,1536]{1,0:T(8,128)(2,1)} %param.26) | copy-start | bytes 9437188
  7.2 63.4 %all-gather.9.cloned.1.call-start = ((), (), s32[]{:S(2)}) async-start(), calls=%async_computation.12 | async-start | bytes 2433024 | tf_op jit(solution)/shard_map/all_gather | solution.py:61
  7.9 123.4 %all-gather.11.cloned.1.call-start = ((), (), s32[]{:S(2)}) async-start(), calls=%async_computation.13 | async-start | bytes 2433024 | tf_op jit(solution)/shard_map/all_gather | solution.py:62
  8.7 189.1 %all-gather.7.cloned.1.call-start = ((), (), s32[]{:S(2)}) async-start(), calls=%async_computation.11 | async-start | bytes 4866048 | tf_op jit(solution)/shard_map/all_gather | solution.py:60
  9.4 253.0 %all-gather.13.cloned.1.call-start = ((), (), s32[]{:S(2)}) async-start(), calls=%async_computation.14 | async-start | bytes 4866048 | tf_op jit(solution)/shard_map/all_gather | solution.py:63
  10.0 293.2 %all-gather.15.cloned.1.call-start = ((), (), s32[]{:S(2)}) async-start(), calls=%async_computation.15 | async-start | bytes 1966080 | tf_op jit(solution)/shard_map/all_gather | solution.py:141
  56.4 14.2 %copy-start.20 = (f32[128]{0:T(128)}, f32[128]{0:T(128)S(1)}, u32[]{:S(2)}) copy-start(f32[128]{0:T(128)S(1)} %get-tuple-element.262) | copy-start | bytes 1540
  70.6 2.9 copy-start.14
  70.6 2.9 copy-start.18
  73.5 57.8 %copy-start.2 = (bf16[128,1536]{1,0:T(8,128)(2,1)S(1)}, bf16[128,1536]{1,0:T(8,128)(2,1)}, u32[]{:S(2)}) copy-start(bf16[128,1536]{1,0:T(8,128)(2,1)} %param.16) | copy-start | bytes 1179652
  197.8 4.3 copy-start.15
  197.8 4.4 copy-start.19
  265.7 0.9 copy-start.3
  266.3 0.5 copy-start.22
  267.7 72.8 %all-gather.17.cloned.1.call-start = ((), (), s32[]{:S(2)}) async-start(), calls=%async_computation.17 | async-start | bytes 1966080 | tf_op jit(solution)/shard_map/all_gather | solution.py:155
  268.3 118.7 %reduce-scatter.18.cloned.1.call-start = ((), (), s32[]{:S(2)}) async-start(), calls=%async_computation.18 | async-start | bytes 1966080 | tf_op jit(solution)/shard_map/reduce_scatter | solution.py:162
  303.2 5.7 copy-start.26
  303.2 5.7 copy-start.28
  340.6 6.3 copy-start.25
  346.9 1.9 copy-start.31
  346.9 1.9 copy-start.29
  346.9 2.6 copy-start.27
  352.6 71.1 %reduce-scatter.16.cloned.1.call-start = ((), (), s32[]{:S(2)}) async-start(), calls=%async_computation.16 | async-start | bytes 1966080 | tf_op jit(solution)/shard_map/reduce_scatter | solution.py:147
  356.8 66.8 %copy-start.4 = (f32[128,1536]{1,0:T(8,128)S(1)}, f32[128,1536]{1,0:T(8,128)}, u32[]{:S(2)}) copy-start(f32[128,1536]{1,0:T(8,128)} %copy-done.3) | copy-start | bytes 2359300
  356.8 66.8 %copy-start.10 = (bf16[128,1536]{1,0:T(8,128)(2,1)S(1)}, bf16[128,1536]{1,0:T(8,128)(2,1)}, u32[]{:S(2)}) copy-start(bf16[128,1536]{1,0:T(8,128)(2,1)} %param.27) | copy-start | bytes 1179652
  356.8 66.8 %copy-start.23 = (f32[128]{0:T(128)S(1)}, f32[128]{0:T(128)}, u32[]{:S(2)}) copy-start(f32[128]{0:T(128)} %copy-done.22) | copy-start | bytes 1540
  356.9 66.8 %copy-start.24 = (f32[128]{0:T(128)S(1)}, f32[128]{0:T(128)}, u32[]{:S(2)}) copy-start(f32[128]{0:T(128)} %get-tuple-element.263) | copy-start | bytes 1540
  356.9 159.9 %reduce-scatter.34.cloned.1.call-start = ((), (), s32[]{:S(2)}) async-start(), calls=%async_computation.26 | async-start | bytes 983040
  425.8 126.8 %copy-start.5 = (f32[128,1536]{1,0:T(8,128)}, f32[128,1536]{1,0:T(8,128)S(1)}, u32[]{:S(2)}) copy-start(f32[128,1536]{1,0:T(8,128)S(1)} %get-tuple-element.252) | copy-start | bytes 2359300
  425.9 4.8 copy-start.8
  492.2 2.5 copy-start.13
  492.2 4.0 copy-start.32
  494.6 47.0 %reduce-scatter.36.cloned.1.call-start = ((), (), s32[]{:S(2)}) async-start(), calls=%async_computation.27 | async-start | bytes 983040
  495.9 117.2 %reduce-scatter.28.cloned.1.call-start = ((), (), s32[]{:S(2)}) async-start(), calls=%async_computation.23 | async-start | bytes 7077888 | tf_op jit(solution)/shard_map/reduce_scatter | solution.py:264
  502.0 1.2 copy-start.30
  502.1 171.7 %reduce-scatter.30.cloned.1.call-start = ((), (), s32[]{:S(2)}) async-start(), calls=%async_computation.24 | async-start | bytes 7077888 | tf_op jit(solution)/shard_map/reduce_scatter | solution.py:265
  509.2 1.2 copy-start.33
  509.2 230.3 %reduce-scatter.32.cloned.1.call-start = ((), (), s32[]{:S(2)}) async-start(), calls=%async_computation.25 | async-start | bytes 7077888 | tf_op jit(solution)/shard_map/reduce_scatter | solution.py:266
  516.4 1.5 copy-start.16
  516.4 1.5 copy-start.17
  516.4 1.6 copy-start.21
  516.4 336.5 %reduce-scatter.22.cloned.1.call-start = ((), (), s32[]{:S(2)}) async-start(), calls=%async_computation.20 | async-start | bytes 4866048 | tf_op jit(solution)/shard_map/reduce_scatter | solution.py:257
  521.1 444.3 %reduce-scatter.24.cloned.1.call-start = ((), (), s32[]{:S(2)}) async-start(), calls=%async_computation.21 | async-start | bytes 4866048 | tf_op jit(solution)/shard_map/reduce_scatter | solution.py:258
  545.6 1.1 copy-start.12
  545.6 561.4 %reduce-scatter.20.cloned.1.call-start = ((), (), s32[]{:S(2)}) async-start(), calls=%async_computation.19 | async-start | bytes 9732096 | tf_op jit(solution)/shard_map/reduce_scatter | solution.py:256
  552.3 1.1 copy-start.9
  552.3 696.1 %reduce-scatter.26.cloned.1.call-start = ((), (), s32[]{:S(2)}) async-start(), calls=%async_computation.22 | async-start | bytes 9732096 | tf_op jit(solution)/shard_map/reduce_scatter | solution.py:259
  559.2 4.4 copy-start.7
  563.6 1.7 copy-start.6
  563.6 1.7 copy-start.11
  565.3 683.2 %copy-start.1 = (bf16[1024,1536]{1,0:T(8,128)(2,1)S(1)}, bf16[1024,1536]{1,0:T(8,128)(2,1)}, u32[]{:S(2)}) copy-start(bf16[1024,1536]{1,0:T(8,128)(2,1)} %param.26) | copy-start | bytes 9437188
Sparse Core Ops, SparseCore 0:
  10.8 59.7 all-gather.8
  73.4 57.8 all-gather.10
  134.1 63.6 all-gather.6
  200.4 61.8 all-gather.12
  267.8 35.3 all-gather.14
  304.6 35.8 all-gather.16
  352.7 34.3 reduce-scatter.17
  389.3 34.2 reduce-scatter.15
  494.7 21.9 reduce-scatter.33
  518.9 22.6 reduce-scatter.35
  545.6 62.3 reduce-scatter.27
  611.8 61.9 reduce-scatter.29
  677.7 61.7 reduce-scatter.31
  745.4 107.5 reduce-scatter.21
  858.9 106.5 reduce-scatter.23
  971.8 135.1 reduce-scatter.19
  1113.3 135.1 reduce-scatter.25
where the time goes:
time: 1260 us; the launch traced here: 1250 us
  waiting for transfers between devices  878 us (70%)
  matrix products  164 us (13%)
  blocking collectives  123 us (10%)
  local copies, waits for them, and re-layouts  51.5 us (4%)
  other arithmetic  21.7 us (2%)
  between operations  14.4 us (1%)
    reduce_scatter x1, waiting for transfers between devices, shards(): lax.psum_scatter(grad_query, ('dp', 'tensor'), scatter_dimension=0, tiled...  142 us
    reduce_scatter x1, waiting for transfers between devices, shards(): lax.psum_scatter(grad_output, ('dp', 'tensor'), scatter_dimension=0, tile...  141 us
    reduce_scatter x1, waiting for transfers between devices, shards(): lax.psum_scatter(grad_key, ('dp', 'tensor'), scatter_dimension=0, tiled=T...  113 us
    reduce_scatter x1, waiting for transfers between devices, shards(): lax.psum_scatter(grad_value, ('dp', 'tensor'), scatter_dimension=0, tiled...  112 us
    unnamed x2, blocking collectives  82.4 us
    reduce_scatter x1, waiting for transfers between devices, shards(): lax.psum_scatter(grad_down, 'dp', scatter_dimension=1, tiled=True)  65.7 us
    reduce_scatter x1, waiting for transfers between devices, shards(): lax.psum_scatter(grad_up, 'dp', scatter_dimension=0, tiled=True)  60.7 us
    all_gather x1, waiting for transfers between devices, shards(): lax.all_gather(w_query, ('dp', 'tensor'), axis=0, tiled=True)  38.5 us
  transfers between devices with their start and end apart: 17, of which 16 were waited for; matrix products, arithmetic and copies ran while one was open for 12% of the time, Pallas kernels for 0%

commit v1 on v0

--- a/solution.py
+++ b/solution.py
@@ -10,6 +10,24 @@
 EPSILON = 1e-05
 ROPE_BASE = 100000.0
 MASKED = -1e30
+
+
+def ring_gather(value, axis, dim):
+    ways, here, turn = (lax.axis_size(axis), lax.axis_index(axis), value.shape[dim])
+    dims = [n * ways if d == dim else n for d, n in enumerate(value.shape)]
+    full = lax.dynamic_update_slice_in_dim(
+        jnp.zeros(dims, value.dtype), value, here * turn, axis=dim
+    )
+    going_up = going_down = value
+    for far in range(1, ways // 2 + 1):
+        going_up = lax.ppermute(going_up, axis, [(d, (d + 1) % ways) for d in range(ways)])
+        full = lax.dynamic_update_slice_in_dim(full, going_up, (here - far) % ways * turn, axis=dim)
+        if 2 * far < ways:
+            going_down = lax.ppermute(going_down, axis, [(d, (d - 1) % ways) for d in range(ways)])
+            full = lax.dynamic_update_slice_in_dim(
+                full, going_down, (here + far) % ways * turn, axis=dim
+            )
+    return full
 
 
 def angle_tables(pos_rows, head_size):
@@ -152,7 +170,7 @@
     ).astype(jnp.float32)
     layer_out = (resid_sum + mlp_sum).astype(jnp.bfloat16)
     grad_float = cotangent.astype(jnp.float32)
-    grad_all = lax.all_gather(cotangent, "tensor", axis=0, tiled=True)
+    grad_all = ring_gather(cotangent, "tensor", 0)
     grad_down = jnp.einsum("sf,sd->fd", act_low, grad_all, preferred_element_type=jnp.float32)
     g_act = jnp.einsum("sd,fd->sf", grad_all, w_down, preferred_element_type=jnp.float32)
     g_gate = (g_act * up_val * sig_gate * (1.0 + gate_val * (1.0 - sig_gate))).astype(jnp.bfloat16)

time: 1260 us -> 1240 us (0.984)
  waiting for transfers between devices: 878 us -> 856 us
    ppermute x0 -> x3, waiting for transfers between devices: none -> 37.9 us  [the longest x1 20.6 us: ring_gather(): lax.ppermute(going_down, axis, [(d, (d - 1) % ways) for d in range(ways)])]
    all_gather x1, waiting for transfers between devices: 34.7 us -> 3.98 us  [shards(): rows_all = lax.all_gather(normed_two, 'tensor', axis=0, tiled=True)]
    all_gather x1 -> x0, waiting for transfers between devices: 28.6 us -> none  [shards(): grad_all = lax.all_gather(cotangent, 'tensor', axis=0, tiled=True)]
  transfers between devices with their start and end apart: 17 -> 19, of which waited for: 16 -> 18; matrix products, arithmetic and copies ran while one was open for 12% -> 12% of each run, Pallas kernels for 0% -> 0%
where the time goes in v1:
time: 1240 us
  waiting for transfers between devices  856 us (69%)
  matrix products  160 us (13%)
  blocking collectives  123 us (10%)
  local copies, waits for them, and re-layouts  58.1 us (5%)
  other arithmetic  21.6 us (2%)
  between operations  14.4 us (1%)
    reduce_scatter x1, waiting for transfers between devices, shards(): lax.psum_scatter(grad_query, ('dp', 'tensor'), scatter_dimension=0, tiled...  142 us
    reduce_scatter x1, waiting for transfers between devices, shards(): lax.psum_scatter(grad_output, ('dp', 'tensor'), scatter_dimension=0, tile...  141 us
    reduce_scatter x1, waiting for transfers between devices, shards(): lax.psum_scatter(grad_key, ('dp', 'tensor'), scatter_dimension=0, tiled=T...  114 us
    reduce_scatter x1, waiting for transfers between devices, shards(): lax.psum_scatter(grad_value, ('dp', 'tensor'), scatter_dimension=0, tiled...  112 us
    unnamed x2, blocking collectives  82.4 us
    reduce_scatter x1, waiting for transfers between devices, shards(): lax.psum_scatter(grad_down, 'dp', scatter_dimension=1, tiled=True)  65.6 us
    reduce_scatter x1, waiting for transfers between devices, shards(): lax.psum_scatter(grad_up, 'dp', scatter_dimension=0, tiled=True)  60.7 us
    all_gather x1, waiting for transfers between devices, shards(): lax.all_gather(w_query, ('dp', 'tensor'), axis=0, tiled=True)  38.5 us
  transfers between devices with their start and end apart: 19, of which 18 were waited for; matrix products, arithmetic and copies ran while one was open for 12% of the time, Pallas kernels for 0%

profile of v1, /device:TPU:0, one launch (start us, length us, event | category | flops | bytes accessed | tf_op | source)
XLA Modules:
  0.0 1240.9 jit_solution(2068072983018890646)
XLA Ops:
  12.6 42.1 %all-reduce.5 = (bf16[1536]{0:T(1024)(128)(2,1)S(1)}, bf16[1536]{0:T(1024)(128)(2,1)S(1)}) all-reduce(bf16[1536]{0:T(1024)(128)(2,1)S(1)} %dynamic-update-slice, bf16[1536]{0:T(1024)(128)(2,1)S(1)} %dynamic-update-slice.1), channel_id=1, replica_groups=mesh['dp'=8,'tensor'=4] {'dp','tensor'}, use_global_device_ids=true, to_apply=%add | all-reduce | flops 3072 | bytes 12288
  58.7 11.9 all-gather.8.cloned.1.call-done
  70.7 2.9 fusion.76
  73.7 19.5 %all_gather.30 = bf16[512,768]{0,1:T(8,128)(2,1)} all-gather(bf16[128,768]{0,1:T(8,128)(2,1)S(1)} %bitcast.215), channel_id=1, replica_groups=mesh['dp'=8,'tensor'=4] {'tensor'}, dimensions={0}, use_global_device_ids=true | all-gather | bytes 983040 | tf_op jit(solution)/shard_map/all_gather | solution.py:106
  93.1 2.2 copy.56
  95.4 35.9 %all-gather.10.cloned.1.call-done = bf16[1536,768]{1,0:T(8,128)(2,1)} async-done(((bf16[48,768]{1,0:T(8,128)(2,1)}), bf16[1536,768]{1,0:T(8,128)(2,1)}) %all-gather.10.cloned.1.call-update) | async-done | bytes 2359312 | tf_op jit(solution)/shard_map/all_gather | solution.py:80
  131.3 2.2 convolution_convert_fusion.2
  133.5 21.3 %all_gather.32 = bf16[512,768]{1,0:T(8,128)(2,1)} all-gather(bf16[128,768]{1,0:T(8,128)(2,1)S(1)} %convolution_convert_fusion.2), channel_id=1, replica_groups=mesh['dp'=8,'tensor'=4] {'tensor'}, dimensions={0}, use_global_device_ids=true | all-gather | bytes 983040 | tf_op jit(solution)/shard_map/all_gather | solution.py:107
  154.8 2.3 copy.55
  157.1 2.2 copy.57
  159.3 38.5 %all-gather.6.cloned.1.call-done = bf16[1536,1536]{1,0:T(8,128)(2,1)} async-done(((bf16[48,1536]{1,0:T(8,128)(2,1)}), bf16[1536,1536]{1,0:T(8,128)(2,1)}) %all-gather.6.cloned.1.call-update) | async-done | bytes 4718608 | tf_op jit(solution)/shard_map/all_gather | solution.py:78
  197.8 4.3 fusion.78
  203.0 2.0 copy.53
  205.0 48.8 %while.30 = (s32[]{:T(128)}, bf16[8,256,96]{1,2,0:T(8,128)(2,1)}, f32[8,256]{1,0:T(8,128)}, bf16[8,256,96]{2,1,0:T(8,128)(2,1)}, bf16[8,512,96]{2,1,0:T(8,128)(2...) while((s32[]{:T(128)}, bf16[8,256,96]{1,2,0:T(8,128)(2,1)}, ...), condition=%wide.region_4.5_spmd.clone.clone, body=%wide.region_1.4_spmd.clone.sunk.clone | while | flops 51379968 | bytes 2338905 | solution.py:154
  207.4 1.9 fusion.160
  213.5 1.8 fusion.160
  219.6 1.8 fusion.160
  225.7 1.8 fusion.160
  231.8 1.9 fusion.160
  237.9 1.8 fusion.160
  244.0 1.8 fusion.160
  250.1 1.8 fusion.160
  253.9 1.8 convert_element_type.118
  255.7 1.8 copy.58
  257.5 4.9 all-gather.12.cloned.1.call-done
  262.4 3.4 multiply_reduce_fusion.1
  269.2 2.4 collective-permute-start.1
  273.0 1.8 constant_dynamic-update-slice_fusion.3
  274.7 10.7 collective-permute-done
  285.5 2.1 collective-permute-start.2
  287.6 1.8 constant_dynamic-update-slice_fusion.2
  289.4 20.6 %collective-permute-done.1 = bf16[128,1536]{1,0:T(8,128)(2,1)} collective-permute-done((bf16[128,1536]{1,0:T(8,128)(2,1)}, bf16[128,1536]{1,0:T(8,128)(2,1)}, u32[]{:S(2)}, u32[]{:S(2)}) %collective-permute-start.1) | collective-permute-done | bytes 393248 | tf_op jit(solution)/shard_map/ppermute | solution.py:26
  311.7 6.6 collective-permute-done.2
  319.1 4.0 all-gather.14.cloned.1.call-done
  323.1 4.3 fusion.81
  329.3 5.1 multiply_convert_fusion.1
  334.4 1.8 fusion.83
  336.2 3.0 fusion.46
  339.3 4.1 convolution_convert_fusion
  343.6 29.1 %reduce-scatter.18.cloned.1.call-done = bf16[128,1536]{1,0:T(8,128)(2,1)} async-done(((bf16[512,1536]{1,0:T(8,128)(2,1)}), bf16[128,1536]{1,0:T(8,128)(2,1)}) %reduce-scatter.18.cloned.1.call-update) | async-done | bytes 393232 | tf_op jit(solution)/shard_map/reduce_scatter | solution.py:180
  372.7 2.1 fusion.54
  374.8 34.5 %reduce-scatter.16.cloned.1.call-done = bf16[128,1536]{1,0:T(8,128)(2,1)} async-done(((bf16[512,1536]{1,0:T(8,128)(2,1)}), bf16[128,1536]{1,0:T(8,128)(2,1)}) %reduce-scatter.16.cloned.1.call-update) | async-done | bytes 393232 | tf_op jit(solution)/shard_map/reduce_scatter | solution.py:165
  409.3 2.2 fusion.51
  411.5 4.3 convolution_convert_fusion.1
  416.3 61.5 %while.31 = (s32[]{:T(128)}, f32[8,256,96]{1,2,0:T(8,128)}, bf16[8,512,96]{1,2,0:T(8,128)(2,1)}, bf16[8,512,96]{1,2,0:T(8,128)(2,1)}, bf16[8,256,96]{2,1,0:T(8,1...) while((s32[]{:T(128)}, f32[8,256,96]{1,2,0:T(8,128)}, ...), condition=%wide.region_11.12_spmd.clone.clone, body=%wide.region_9.11_spmd.clone.sunk.clone | while | flops 127082240 | bytes 5417073 | solution.py:230
  477.8 2.4 copy.68
  481.8 5.9 fusion.85
  488.9 5.9 fusion.86
  496.1 6.0 fusion.87
  503.7 3.1 fusion.71
  506.8 20.6 %reduce-scatter.36.cloned.1.call-done = bf16[128,768]{1,0:T(8,128)(2,1)} async-done(((bf16[512,768]{1,0:T(8,128)(2,1)}), bf16[128,768]{1,0:T(8,128)(2,1)}) %reduce-scatter.36.cloned.1.call-update) | async-done | bytes 196624
  527.4 3.9 fusion.69
  532.7 5.5 fusion.73
  539.2 5.8 fusion.64
  545.1 4.3 fusion.84
  551.1 2.5 fusion.62
  553.5 40.2 %all-reduce.4 = (f32[1536]{0:T(1024)}, f32[1536]{0:T(1024)}) all-reduce(f32[1536]{0:T(1024)} %get-tuple-element.201, f32[1536]{0:T(1024)} %get-tuple-element.199), channel_id=6, replica_groups=mesh['dp'=8,'tensor'=4] {'dp','tensor'}, use_global_device_ids=true, to_apply=%region_16.17.clone | all-reduce | flops 3072 | bytes 24576
  596.3 2.5 fusion.59
  598.9 60.7 %reduce-scatter.30.cloned.1.call-done = f32[192,1024]{1,0:T(8,128)} async-done(((f32[1536,1024]{1,0:T(8,128)}), f32[192,1024]{1,0:T(8,128)}) %reduce-scatter.30.cloned.1.call-update) | async-done | bytes 786448 | tf_op jit(solution)/shard_map/reduce_scatter | solution.py:283
  659.5 65.6 %reduce-scatter.32.cloned.1.call-done = f32[1024,192]{0,1:T(8,128)} async-done(((f32[1024,1536]{0,1:T(8,128)}), f32[1024,192]{0,1:T(8,128)}) %reduce-scatter.32.cloned.1.call-update) | async-done | bytes 786448 | tf_op jit(solution)/shard_map/reduce_scatter | solution.py:284
  725.1 113.8 %reduce-scatter.22.cloned.1.call-done = f32[48,768]{1,0:T(8,128)} async-done(((f32[1536,768]{1,0:T(8,128)}), f32[48,768]{1,0:T(8,128)}) %reduce-scatter.22.cloned.1.call-update) | async-done | bytes 147472 | tf_op jit(solution)/shard_map/reduce_scatter | solution.py:275
  838.9 112.3 %reduce-scatter.24.cloned.1.call-done = f32[48,768]{1,0:T(8,128)} async-done(((f32[1536,768]{1,0:T(8,128)}), f32[48,768]{1,0:T(8,128)}) %reduce-scatter.24.cloned.1.call-update) | async-done | bytes 147472 | tf_op jit(solution)/shard_map/reduce_scatter | solution.py:276
  951.2 141.7 %reduce-scatter.20.cloned.1.call-done = f32[48,1536]{1,0:T(8,128)} async-done(((f32[1536,1536]{1,0:T(8,128)}), f32[48,1536]{1,0:T(8,128)}) %reduce-scatter.20.cloned.1.call-update) | async-done | bytes 294928 | tf_op jit(solution)/shard_map/reduce_scatter | solution.py:274
  1092.9 141.5 %reduce-scatter.26.cloned.1.call-done = f32[48,1536]{1,0:T(8,128)} async-done(((f32[1536,1536]{1,0:T(8,128)}), f32[48,1536]{1,0:T(8,128)}) %reduce-scatter.26.cloned.1.call-update) | async-done | bytes 294928 | tf_op jit(solution)/shard_map/reduce_scatter | solution.py:277
  (248 shorter events, 127.5 us)
Async XLA Ops:
  7.2 322.1 %copy-start = (bf16[1024,1536]{1,0:T(8,128)(2,1)S(1)}, bf16[1024,1536]{1,0:T(8,128)(2,1)}, u32[]{:S(2)}) copy-start(bf16[1024,1536]{1,0:T(8,128)(2,1)} %param.26) | copy-start | bytes 9437188
  7.2 63.4 %all-gather.8.cloned.1.call-start = ((), (), s32[]{:S(2)}) async-start(), calls=%async_computation.12 | async-start | bytes 2433024 | tf_op jit(solution)/shard_map/all_gather | solution.py:79
  7.9 123.4 %all-gather.10.cloned.1.call-start = ((), (), s32[]{:S(2)}) async-start(), calls=%async_computation.13 | async-start | bytes 2433024 | tf_op jit(solution)/shard_map/all_gather | solution.py:80
  8.7 189.1 %all-gather.6.cloned.1.call-start = ((), (), s32[]{:S(2)}) async-start(), calls=%async_computation.11 | async-start | bytes 4866048 | tf_op jit(solution)/shard_map/all_gather | solution.py:78
  9.4 253.0 %all-gather.12.cloned.1.call-start = ((), (), s32[]{:S(2)}) async-start(), calls=%async_computation.14 | async-start | bytes 4866048 | tf_op jit(solution)/shard_map/all_gather | solution.py:81
  10.0 313.1 %all-gather.14.cloned.1.call-start = ((), (), s32[]{:S(2)}) async-start(), calls=%async_computation.15 | async-start | bytes 1966080 | tf_op jit(solution)/shard_map/all_gather | solution.py:159
  56.4 14.2 %copy-start.20 = (f32[128]{0:T(128)}, f32[128]{0:T(128)S(1)}, u32[]{:S(2)}) copy-start(f32[128]{0:T(128)S(1)} %get-tuple-element.262) | copy-start | bytes 1540
  70.6 2.9 copy-start.14
  70.6 2.9 copy-start.18
  73.5 57.8 %copy-start.2 = (bf16[128,1536]{1,0:T(8,128)(2,1)S(1)}, bf16[128,1536]{1,0:T(8,128)(2,1)}, u32[]{:S(2)}) copy-start(bf16[128,1536]{1,0:T(8,128)(2,1)} %param.16) | copy-start | bytes 1179652
  197.8 4.3 copy-start.15
  197.8 4.4 copy-start.19
  265.7 0.9 copy-start.3
  266.3 0.5 copy-start.22
  267.7 104.9 %reduce-scatter.18.cloned.1.call-start = ((), (), s32[]{:S(2)}) async-start(), calls=%async_computation.17 | async-start | bytes 1966080 | tf_op jit(solution)/shard_map/reduce_scatter | solution.py:180
  267.8 17.7 %collective-permute-start = (bf16[128,1536]{1,0:T(8,128)(2,1)}, bf16[128,1536]{1,0:T(8,128)(2,1)}, u32[]{:S(2)}, u32[]{:S(2)}) collective-permute-start(bf16[128,1536]{1,0:T(8,128)(2,1)} %param.27), channel_id=1, source_target_pairs={{0,1},{1,2},{2,3},{3,0},{4,5},{5,6},{6,7},{7,4},{8,9},{9,10},{10,1... | collective-permute-start | bytes 1179656 | tf_op jit(solution)/shard_map/ppermute | solution.py:23
  269.2 40.7 %collective-permute-start.1 = (bf16[128,1536]{1,0:T(8,128)(2,1)}, bf16[128,1536]{1,0:T(8,128)(2,1)}, u32[]{:S(2)}, u32[]{:S(2)}) collective-permute-start(bf16[128,1536]{1,0:T(8,128)(2,1)} %param.27), channel_id=1, source_target_pairs={{0,3},{1,0},{2,1},{3,2},{4,7},{5,4},{6,5},{7,6},{8,11},{9,8},{10,9... | collective-permute-start | bytes 1179656 | tf_op jit(solution)/shard_map/ppermute | solution.py:26
  285.5 32.9 %collective-permute-start.2 = (bf16[128,1536]{1,0:T(8,128)(2,1)}, bf16[128,1536]{1,0:T(8,128)(2,1)S(1)}, u32[]{:S(2)}, u32[]{:S(2)}) collective-permute-start(bf16[128,1536]{1,0:T(8,128)(2,1)} %collective-permute-done), channel_id=1, source_target_pairs={{0,1},{1,2},{2,3},{3,0},{4,5},{5,6},{6,7},{7,4},{8,9},{9,10},{10,1... | collective-permute-start | bytes 1179656 | tf_op jit(solution)/shard_map/ppermute | solution.py:23
  323.1 4.3 copy-start.26
  323.1 4.3 copy-start.27
  329.3 5.1 copy-start.25
  334.4 1.8 copy-start.30
  334.4 1.9 copy-start.28
  339.2 70.0 %reduce-scatter.16.cloned.1.call-start = ((), (), s32[]{:S(2)}) async-start(), calls=%async_computation.16 | async-start | bytes 1966080 | tf_op jit(solution)/shard_map/reduce_scatter | solution.py:165
  343.4 65.9 %copy-start.4 = (f32[128,1536]{1,0:T(8,128)S(1)}, f32[128,1536]{1,0:T(8,128)}, u32[]{:S(2)}) copy-start(f32[128,1536]{1,0:T(8,128)} %copy-done.3) | copy-start | bytes 2359300
  343.4 65.9 %copy-start.10 = (bf16[128,1536]{1,0:T(8,128)(2,1)S(1)}, bf16[128,1536]{1,0:T(8,128)(2,1)}, u32[]{:S(2)}) copy-start(bf16[128,1536]{1,0:T(8,128)(2,1)} %param.27) | copy-start | bytes 1179652
  343.4 65.9 %copy-start.23 = (f32[128]{0:T(128)S(1)}, f32[128]{0:T(128)}, u32[]{:S(2)}) copy-start(f32[128]{0:T(128)} %copy-done.22) | copy-start | bytes 1540
  343.5 65.9 %copy-start.24 = (f32[128]{0:T(128)S(1)}, f32[128]{0:T(128)}, u32[]{:S(2)}) copy-start(f32[128]{0:T(128)} %get-tuple-element.263) | copy-start | bytes 1540
  343.5 158.9 %reduce-scatter.34.cloned.1.call-start = ((), (), s32[]{:S(2)}) async-start(), calls=%async_computation.25 | async-start | bytes 983040
  411.5 127.0 %copy-start.5 = (f32[128,1536]{1,0:T(8,128)}, f32[128,1536]{1,0:T(8,128)S(1)}, u32[]{:S(2)}) copy-start(f32[128,1536]{1,0:T(8,128)S(1)} %get-tuple-element.252) | copy-start | bytes 2359300
  411.5 4.8 copy-start.8
  477.8 2.5 copy-start.13
  477.8 4.0 copy-start.31
  480.2 47.2 %reduce-scatter.36.cloned.1.call-start = ((), (), s32[]{:S(2)}) async-start(), calls=%async_computation.26 | async-start | bytes 983040
  481.5 117.4 %reduce-scatter.28.cloned.1.call-start = ((), (), s32[]{:S(2)}) async-start(), calls=%async_computation.22 | async-start | bytes 7077888 | tf_op jit(solution)/shard_map/reduce_scatter | solution.py:282
  487.7 1.2 copy-start.29
  487.7 171.8 %reduce-scatter.30.cloned.1.call-start = ((), (), s32[]{:S(2)}) async-start(), calls=%async_computation.23 | async-start | bytes 7077888 | tf_op jit(solution)/shard_map/reduce_scatter | solution.py:283
  494.8 1.2 copy-start.32
  494.8 230.2 %reduce-scatter.32.cloned.1.call-start = ((), (), s32[]{:S(2)}) async-start(), calls=%async_computation.24 | async-start | bytes 7077888 | tf_op jit(solution)/shard_map/reduce_scatter | solution.py:284
  502.0 1.5 copy-start.16
  502.0 1.5 copy-start.17
  502.0 1.6 copy-start.21
  502.0 336.8 %reduce-scatter.22.cloned.1.call-start = ((), (), s32[]{:S(2)}) async-start(), calls=%async_computation.19 | async-start | bytes 4866048 | tf_op jit(solution)/shard_map/reduce_scatter | solution.py:275
  506.8 444.4 %reduce-scatter.24.cloned.1.call-start = ((), (), s32[]{:S(2)}) async-start(), calls=%async_computation.20 | async-start | bytes 4866048 | tf_op jit(solution)/shard_map/reduce_scatter | solution.py:276
  531.3 1.1 copy-start.12
  531.4 561.5 %reduce-scatter.20.cloned.1.call-start = ((), (), s32[]{:S(2)}) async-start(), calls=%async_computation.18 | async-start | bytes 9732096 | tf_op jit(solution)/shard_map/reduce_scatter | solution.py:274
  538.2 1.0 copy-start.9
  538.2 696.2 %reduce-scatter.26.cloned.1.call-start = ((), (), s32[]{:S(2)}) async-start(), calls=%async_computation.21 | async-start | bytes 9732096 | tf_op jit(solution)/shard_map/reduce_scatter | solution.py:277
  545.1 4.3 copy-start.7
  549.4 1.7 copy-start.6
  549.4 1.7 copy-start.11
  551.1 683.3 %copy-start.1 = (bf16[1024,1536]{1,0:T(8,128)(2,1)S(1)}, bf16[1024,1536]{1,0:T(8,128)(2,1)}, u32[]{:S(2)}) copy-start(bf16[1024,1536]{1,0:T(8,128)(2,1)} %param.26) | copy-start | bytes 9437188
Sparse Core Ops, SparseCore 0:
  10.8 59.7 all-gather.7
  73.4 57.8 all-gather.9
  134.1 63.6 all-gather.5
  200.4 61.8 all-gather.11
  267.8 55.2 all-gather.13
  339.4 33.2 reduce-scatter.17
  375.0 34.2 reduce-scatter.15
  480.4 21.9 reduce-scatter.33
  504.7 22.6 reduce-scatter.35
  531.2 62.1 reduce-scatter.27
  597.4 62.0 reduce-scatter.29
  663.3 61.7 reduce-scatter.31
  731.1 107.6 reduce-scatter.21
  844.8 106.3 reduce-scatter.23
  957.5 135.3 reduce-scatter.19
  1099.2 135.0 reduce-scatter.25
